TPU v7x, 32 devices: a whole 2x2x4 slice. The times are simulated.
32 devices in a mesh: groups: 2 (over y), expert: 8 (over z, x), tensor: 2 (over core).
Axes of the slice: x: 2, y: 2, z: 4, core: 2. Of those that a mesh axis runs over, the one named last changes fastest.
Arguments:
- conv_input: bfloat16 [32, 8192], P(('groups', 'expert'), 'tensor'), parts along dimension 0, may hold values from -6 to 6
- gate_input: bfloat16 [32, 8192], P(('groups', 'expert'), 'tensor'), parts along dimension 0, may hold values from -6 to 6
- step_input: bfloat16 [32, 8192], P(('groups', 'expert'), 'tensor'), parts along dimension 0, may hold values from -6 to 6
- b_proj: float32 [32, 16], P(('groups', 'expert')), parts along dimension 0, may hold values from -6 to 6
- c_proj: float32 [32, 16], P(('groups', 'expert')), parts along dimension 0, may hold values from -6 to 6
- slot_ids: int32 [32], P(('groups', 'expert')), parts along dimension 0, may hold values from 0 to 15, as said below
- state_pool: bfloat16 [32, 16, 8192], P(('groups', 'expert'), None, 'tensor'), parts along dimension 0, may hold values from -6 to 6
- conv_pool: bfloat16 [32, 3, 8192], P(('groups', 'expert'), None, 'tensor'), parts along dimension 0, may hold values from -6 to 6
- conv_weight: float32 [4, 8192], P(None, 'tensor'), may hold values from -4 to 4
- conv_bias: float32 [8192], P('tensor'), may hold values from -4 to 4
- step_bias: float32 [8192], P('tensor'), may hold values from -4 to 0
- a_log: float32 [16, 8192], P(None, 'tensor'), may hold values from -1 to 2.5
- d_skip: float32 [8192], P('tensor'), may hold values from 0.5 to 1.5
- out_weight: bfloat16 [8192, 4096], P('tensor', 'expert'), may hold values from -0.0625 to 0.0625
- residual: bfloat16 [32, 4096], P(('groups', 'expert')), parts along dimension 0, may hold values from -6 to 6
- norm_gain: float32 [4096], replicated, may hold values from 0.5 to 1.5
- expert_ids: int32 [32, 2], P(('groups', 'expert')), parts along dimension 0, may hold values from 0 to 2, all different within a row
- expert_probs: bfloat16 [32, 2], P(('groups', 'expert')), parts along dimension 0, may hold values from 0.19921875 to 1
- gate_weight: bfloat16 [36864, 4096], P(('expert', 'tensor')), may hold values from -0.09375 to 0.09375
- up_weight: bfloat16 [36864, 4096], P(('expert', 'tensor')), may hold values from -0.09375 to 0.09375
- down_weight: bfloat16 [36864, 4096], P(('expert', 'tensor')), may hold values from -0.0546875 to 0.0546875
Outputs:
- layer_out: bfloat16 [32, 4096], P(('groups', 'expert')), parts along dimension 0
- new_state: bfloat16 [32, 16, 8192], P(('groups', 'expert'), None, 'tensor'), parts along dimension 0
There are 2 independent parts, one for each index of `groups`. A program takes and returns all parts, laid end to end along the dimension named above; an argument that names none is the same for every part. Nothing has to cross between parts.
Inputs may be any that keep to these rules, and one draw needn't show every extreme that they name: `slot_ids`: the rows of one index of expert (rows d*2 to (d+1)*2 - 1) use distinct slots among d*2 to (d+1)*2 - 1. `expert_ids`: each row names two different experts.
All inputs are finite; a program needn't handle non-finite values.
Results may differ from a plain program's by a relative error of at most 0.0063.
Values may be sent and summed in bfloat16 or wider, within the bound.
A program may use at most 128 MiB of HBM per device.

v0:
```python
import jax
import jax.numpy as jnp
from jax import lax
from jax.sharding import PartitionSpec as P

EXPERTS = 3
FF = 12288


def mamba_step(
    states,
    history,
    conv_input,
    gate_input,
    step_input,
    b_proj,
    c_proj,
    conv_weight,
    conv_bias,
    step_bias,
    a_log,
    d_skip,
):
    inputs = conv_input.astype(jnp.float32)
    conv_sum = conv_weight[-1] * inputs + conv_bias
    for lag in range(history.shape[1]):
        conv_sum = conv_sum + conv_weight[lag] * history[:, lag]
    conv_out = jax.nn.silu(conv_sum)
    step_size = jax.nn.softplus(step_input.astype(jnp.float32) + step_bias)
    state_rates = -jnp.exp(a_log)
    decay_rate = jnp.exp(step_size[:, None, :] * state_rates[None])
    state_next = decay_rate * states + (step_size * conv_out)[:, None, :] * b_proj[:, :, None]
    output = jnp.sum(c_proj[:, :, None] * state_next, axis=1) + d_skip * conv_out
    gated_out = (output * jax.nn.silu(gate_input.astype(jnp.float32))).astype(jnp.bfloat16)
    return (state_next, gated_out)


def expert_terms(rows, coefs, first_unit, gate_weight, up_weight, down_weight):
    dims = (((1,), (1,)), ((), ()))
    gate_act = lax.dot_general(rows, gate_weight, dims, preferred_element_type=jnp.float32)
    up_act = lax.dot_general(rows, up_weight, dims, preferred_element_type=jnp.float32)
    hidden = (jax.nn.silu(gate_act) * up_act).astype(jnp.bfloat16)
    units = gate_weight.shape[0]
    lower_expert = first_unit // FF
    boundary = (lower_expert + 1) * FF - first_unit
    column = jnp.arange(units, dtype=jnp.int32)[None, :]
    zeros_bf = jnp.zeros_like(hidden)
    lower_hidden = jnp.where(column < boundary, hidden, zeros_bf)
    upper_hidden = jnp.where(column >= boundary, hidden, zeros_bf)
    expert_range = jnp.arange(EXPERTS, dtype=jnp.int32)[None, :]
    wide_coefs = coefs.astype(jnp.float32)
    lower_coef = jnp.sum(wide_coefs * (expert_range == lower_expert).astype(jnp.float32), axis=1)
    upper_coef = jnp.sum(
        wide_coefs * (expert_range == lower_expert + 1).astype(jnp.float32), axis=1
    )
    lower_out = jnp.dot(lower_hidden, down_weight, preferred_element_type=jnp.float32)
    upper_out = jnp.dot(upper_hidden, down_weight, preferred_element_type=jnp.float32)
    return lower_coef[:, None] * lower_out + upper_coef[:, None] * upper_out


def local(
    conv_input,
    gate_input,
    step_input,
    b_proj,
    c_proj,
    slot_ids,
    state_pool,
    conv_pool,
    conv_weight,
    conv_bias,
    step_bias,
    a_log,
    d_skip,
    out_weight,
    residual,
    norm_gain,
    expert_ids,
    expert_probs,
    gate_weight,
    up_weight,
    down_weight,
):
    pool_dev = state_pool.shape[0]
    local_slot = slot_ids - lax.axis_index("expert") * pool_dev
    select = (local_slot[:, None] == jnp.arange(pool_dev, dtype=jnp.int32)[None, :]).astype(
        jnp.bfloat16
    )
    states = jnp.einsum("rp,pnc->rnc", select, state_pool, preferred_element_type=jnp.float32)
    history = jnp.einsum("rp,pkc->rkc", select, conv_pool, preferred_element_type=jnp.float32)
    state_next, gated_out = mamba_step(
        states,
        history,
        conv_input,
        gate_input,
        step_input,
        b_proj,
        c_proj,
        conv_weight,
        conv_bias,
        step_bias,
        a_log,
        d_skip,
    )
    columns = jnp.dot(
        lax.all_gather(gated_out, "expert", axis=0, tiled=True),
        out_weight,
        preferred_element_type=jnp.float32,
    )
    returned_cols = lax.all_to_all(columns, "expert", split_axis=0, concat_axis=1, tiled=True)
    mixed = lax.psum(returned_cols, "tensor").astype(jnp.bfloat16)
    hidden_state = (residual.astype(jnp.float32) + mixed.astype(jnp.float32)).astype(jnp.bfloat16)
    wide = hidden_state.astype(jnp.float32)
    normed = (
        wide * lax.rsqrt(jnp.mean(wide * wide, axis=1, keepdims=True) + 1e-05) * norm_gain
    ).astype(jnp.bfloat16)
    probs = expert_probs.astype(jnp.float32)
    expert_range = jnp.arange(EXPERTS, dtype=jnp.int32)
    picked = (expert_ids[:, :, None] == expert_range[None, None, :]).astype(jnp.float32)
    coefs = jnp.sum(picked * probs[:, :, None], axis=1).astype(jnp.bfloat16)
    units = gate_weight.shape[0]
    first_unit = (
        lax.axis_index("expert") * lax.axis_size("tensor") + lax.axis_index("tensor")
    ) * units
    peers = lax.axis_size("expert")
    span = EXPERTS * FF // peers
    dest = jnp.arange(peers, dtype=jnp.int32)[:, None]
    intersection = (
        (expert_range[None, :] * FF < (dest + 1) * span)
        & ((expert_range[None, :] + 1) * FF > dest * span)
    ).astype(jnp.float32)
    chosen = jnp.sum(picked, axis=1)
    needed = jnp.dot(intersection, chosen.T, preferred_element_type=jnp.float32) > 0.5
    outgoing = jnp.where(needed[:, :, None], normed[None], jnp.zeros_like(normed)[None])
    out_coefs = jnp.broadcast_to(coefs[None], (peers, coefs.shape[0], coefs.shape[1]))
    rows_in = lax.all_to_all(outgoing, "expert", split_axis=0, concat_axis=0, tiled=True)
    coefs_in = lax.all_to_all(out_coefs, "expert", split_axis=0, concat_axis=0, tiled=True)
    flat_rows = rows_in.reshape(-1, rows_in.shape[2])
    flat_coefs = coefs_in.reshape(-1, coefs_in.shape[2])
    result = expert_terms(flat_rows, flat_coefs, first_unit, gate_weight, up_weight, down_weight)
    partial_value = result.reshape(rows_in.shape[0], rows_in.shape[1], rows_in.shape[2])
    returned = lax.all_to_all(partial_value, "expert", split_axis=0, concat_axis=0, tiled=True)
    routed = lax.psum(jnp.sum(returned, axis=0), "tensor")
    layer_out = (hidden_state.astype(jnp.float32) + routed).astype(jnp.bfloat16)
    return (layer_out, state_next.astype(jnp.bfloat16))


def solution(mesh):
    return jax.shard_map(
        local,
        mesh=mesh,
        in_specs=(
            P(("groups", "expert"), "tensor"),
            P(("groups", "expert"), "tensor"),
            P(("groups", "expert"), "tensor"),
            P(("groups", "expert"), None),
            P(("groups", "expert"), None),
            P(("groups", "expert")),
            P(("groups", "expert"), None, "tensor"),
            P(("groups", "expert"), None, "tensor"),
            P(None, "tensor"),
            P("tensor"),
            P("tensor"),
            P(None, "tensor"),
            P("tensor"),
            P("tensor", "expert"),
            P(("groups", "expert"), None),
            P(),
            P(("groups", "expert"), None),
            P(("groups", "expert"), None),
            P(("expert", "tensor"), None),
            P(("expert", "tensor"), None),
            P(("expert", "tensor"), None),
        ),
        out_specs=(P(("groups", "expert"), None), P(("groups", "expert"), None, "tensor")),
        check_vma=False,
    )
```

profile of v0, /device:TPU:0, one launch (start us, length us, event | category | flops | bytes accessed | tf_op | source)
XLA Modules:
  0.0 134.9 jit_solution(396333789273066836)
XLA Ops:
  0.6 0.0 copy-start
  0.7 0.8 copy.73
  1.4 0.8 copy.71
  2.2 1.1 fusion.39
  3.3 1.0 exponential_negate_fusion
  4.3 0.7 broadcast_subtract_fusion
  4.9 1.0 fusion.32
  6.0 0.9 fusion.37
  6.9 0.0 copy-done
  6.9 1.1 fusion.38
  8.0 0.8 fusion.24
  8.8 32.3 %all-gather = bf16[8,2,4096]{2,1,0:T(2,128)(2,1)S(1)} all-gather(bf16[1,2,4096]{2,1,0:T(2,128)(2,1)S(1)} %fusion.24), channel_id=1, replica_groups=mesh['groups'=2,'expert'=8,'tensor'=2] {'expert'}, dimensions={0}, use_global_device_ids=true | all-gather | bytes 147456 | tf_op jit(solution)/shard_map/all_gather | solution.py:106
  41.2 0.1 reshape.106
  41.2 2.8 %fusion.40 = f32[16,512]{1,0:T(8,128)S(1)} fusion(bf16[16,4096]{1,0:T(8,128)(2,1)S(1)} %reshape.106, bf16[4096,512]{1,0:T(8,128)(2,1)} %param.34), kind=kOutput, calls=%fused_computation.76 | convolution fusion | flops 67108864 | bytes 4358144 | tf_op jit(solution)/shard_map/dot_general | solution.py:105
  44.0 0.7 all_to_all.23
  44.7 5.5 %all-to-all-start = ((f32[8,2,512]{2,1,0:T(2,128)}), f32[8,2,512]{2,1,0:T(2,128)S(1)}, u32[]{:S(2)}, u32[]{:S(2)}) async-start(f32[8,2,512]{2,1,0:T(2,128)} %all_to_all.23), calls=%async_computation | async-start | bytes 65536 | tf_op jit(solution)/shard_map/all_to_all | solution.py:110
  50.2 0.7 convert_element_type.85
  50.8 0.8 convert_reduce_fusion
  51.6 0.2 convolution_compare_fusion
  51.8 0.1 copy.77
  51.9 5.0 %all-to-all-done = f32[8,2,512]{2,1,0:T(2,128)S(1)} async-done(((f32[8,2,512]{2,1,0:T(2,128)}), f32[8,2,512]{2,1,0:T(2,128)S(1)}, u32[]{:S(2)}, u32[]{:S(2)}) %all-to-all-start) | async-done | bytes 32800 | tf_op jit(solution)/shard_map/all_to_all | solution.py:110
  56.8 0.6 broadcast_in_dim.29
  57.4 3.3 %all-to-all-start.1 = ((bf16[8,2,3]{2,1,0:T(2,128)(2,1)}), bf16[8,2,3]{2,1,0:T(2,128)(2,1)S(1)}, u32[]{:S(2)}, u32[]{:S(2)}) async-start(bf16[8,2,3]{2,1,0:T(2,128)(2,1)} %broadcast_in_dim.29), calls=%async_computation.1 | async-start | bytes 8192 | tf_op jit(solution)/shard_map/all_to_all | solution.py:137
  60.8 3.4 %psum.14 = bf16[2,4096]{1,0:T(2,128)(2,1)S(1)} all-reduce(f32[2,4096]{1,0:T(2,128)S(1)} %bitcast.56), channel_id=1, replica_groups=mesh['groups'=2,'expert'=8,'tensor'=2] {'tensor'}, use_global_device_ids=true, to_apply=%region_1.2 | all-reduce | flops 8192 | bytes 49152 | tf_op jit(solution)/shard_map/psum | solution.py:111
  64.2 0.9 fusion.13
  65.0 0.8 fusion.15
  65.9 0.8 broadcast_select_fusion
  66.7 0.4 all-to-all-done.1
  67.1 5.5 %all-to-all-start.2 = ((bf16[8,2,4096]{2,1,0:T(2,128)(2,1)}), bf16[8,2,4096]{2,1,0:T(2,128)(2,1)S(1)}, u32[]{:S(2)}, u32[]{:S(2)}) async-start(bf16[8,2,4096]{2,1,0:T(2,128)(2,1)} %broadcast_select_fusion), calls=%async_computation.2 | async-start | bytes 262144 | tf_op jit(solution)/shard_map/all_to_all | solution.py:136
  72.6 0.1 copy.75
  72.7 0.1 fusion.27
  72.8 0.1 copy.78
  72.9 0.1 mul.262
  73.0 0.1 copy.76
  73.1 0.1 mul.245
  73.1 6.9 %all-to-all-done.2 = bf16[8,2,4096]{2,1,0:T(2,128)(2,1)S(1)} async-done(((bf16[8,2,4096]{2,1,0:T(2,128)(2,1)}), bf16[8,2,4096]{2,1,0:T(2,128)(2,1)S(1)}, u32[]{:S(2)}, u32[]{:S(2)}) %all-to-all-start.2) | async-done | bytes 131104 | tf_op jit(solution)/shard_map/all_to_all | solution.py:136
  80.1 0.1 reshape.103
  80.1 11.3 %fusion.41 = f32[16,2304]{1,0:T(8,128)S(1)} fusion(bf16[16,4096]{1,0:T(8,128)(2,1)S(1)} %reshape.103, bf16[2304,4096]{1,0:T(8,128)(2,1)} %param.39), kind=kOutput, calls=%fused_computation.77 | convolution fusion | flops 301989888 | bytes 19152896 | tf_op jit(solution)/shard_map/dot_general | solution.py:40
  91.5 11.3 %fusion.2 = bf16[16,2304]{1,0:T(8,128)(2,1)S(1)} fusion(bf16[16,4096]{1,0:T(8,128)(2,1)S(1)} %reshape.103, bf16[2304,4096]{1,0:T(8,128)(2,1)} %param.40, f32[16,2304]{1,0:T(8,128)S(1)} %fusion.41), kind=kOutput, calls=%fused_computation.6 | convolution fusion | flops 302211072 | bytes 19226624 | tf_op jit(solution)/shard_map/dot_general | solution.py:41
  102.8 7.7 %convolution_multiply_fusion.2 = f32[16,4096]{1,0:T(8,128)S(1)} fusion(bf16[2304,4096]{1,0:T(8,128)(2,1)} %param.41, f32[16]{0:T(128)S(1)} %mul.245, bf16[16,2304]{1,0:T(8,128)(2,1)S(1)} %fusion.2, pred[2304]{0:T(1024)(128)(4,1)S(1)} %get-tuple-element.38), kind=kOutput, calls=%fused_computation.4 | convolution fusion | flops 302092288 | bytes 19212608 | tf_op jit(solution)/shard_map/dot_general | solution.py:56
  110.5 7.7 %fusion.1 = f32[16,4096]{1,0:T(8,128)S(1)} fusion(f32[16,4096]{1,0:T(8,128)S(1)} %convolution_multiply_fusion.2, bf16[2304,4096]{1,0:T(8,128)(2,1)} %param.41, f32[16]{0:T(128)S(1)} %mul.262, bf16[16,2304]{1,0:T(8,128)(2,1)S(1)} %fusion.2, pred[2304]{0:T(1024)(128)(4,1)S(1)} %get-tuple-element.37), kind=kOutput, calls=%fused_computation.3 | convolution fusion | flops 302157824 | bytes 19474752 | tf_op jit(solution)/shard_map/dot_general | solution.py:57
  118.2 0.8 reshape.104
  119.1 3.4 %all-to-all-start.3 = ((f32[8,2,4096]{2,1,0:T(2,128)}), f32[8,2,4096]{2,1,0:T(2,128)S(1)}, u32[]{:S(2)}, u32[]{:S(2)}) async-start(f32[8,2,4096]{2,1,0:T(2,128)} %reshape.104), calls=%async_computation.3 | async-start | bytes 524288 | tf_op jit(solution)/shard_map/all_to_all | solution.py:142
  122.5 0.9 copy.79
  123.4 7.4 %all-to-all-done.3 = f32[8,2,4096]{2,1,0:T(2,128)S(1)} async-done(((f32[8,2,4096]{2,1,0:T(2,128)}), f32[8,2,4096]{2,1,0:T(2,128)S(1)}, u32[]{:S(2)}, u32[]{:S(2)}) %all-to-all-start.3) | async-done | bytes 262176 | tf_op jit(solution)/shard_map/all_to_all | solution.py:142
  130.8 0.1 reduce_sum.69
  130.9 3.4 %psum.15 = f32[2,4096]{1,0:T(2,128)S(1)} all-reduce(f32[2,4096]{1,0:T(2,128)S(1)} %reduce_sum.69), channel_id=1, replica_groups=mesh['groups'=2,'expert'=8,'tensor'=2] {'tensor'}, use_global_device_ids=true, to_apply=%region_8.9 | all-reduce | flops 8192 | bytes 65536 | tf_op jit(solution)/shard_map/psum | solution.py:143
  134.3 0.6 fusion.16
  (5 shorter events, 0.0 us)
Async XLA Ops:
  0.6 6.3 %copy-start = (bf16[2,16,4096]{2,1,0:T(8,128)(2,1)S(1)}, bf16[2,16,4096]{2,1,0:T(8,128)(2,1)}, u32[]{:S(2)}) copy-start(bf16[2,16,4096]{2,1,0:T(8,128)(2,1)} %param.27) | copy-start | bytes 786436
  44.7 12.1 %all-to-all-start = ((f32[8,2,512]{2,1,0:T(2,128)}), f32[8,2,512]{2,1,0:T(2,128)S(1)}, u32[]{:S(2)}, u32[]{:S(2)}) async-start(f32[8,2,512]{2,1,0:T(2,128)} %all_to_all.23), calls=%async_computation | async-start | bytes 65536 | tf_op jit(solution)/shard_map/all_to_all | solution.py:110
  57.4 9.7 %all-to-all-start.1 = ((bf16[8,2,3]{2,1,0:T(2,128)(2,1)}), bf16[8,2,3]{2,1,0:T(2,128)(2,1)S(1)}, u32[]{:S(2)}, u32[]{:S(2)}) async-start(bf16[8,2,3]{2,1,0:T(2,128)(2,1)} %broadcast_in_dim.29), calls=%async_computation.1 | async-start | bytes 8192 | tf_op jit(solution)/shard_map/all_to_all | solution.py:137
  67.1 13.0 %all-to-all-start.2 = ((bf16[8,2,4096]{2,1,0:T(2,128)(2,1)}), bf16[8,2,4096]{2,1,0:T(2,128)(2,1)S(1)}, u32[]{:S(2)}, u32[]{:S(2)}) async-start(bf16[8,2,4096]{2,1,0:T(2,128)(2,1)} %broadcast_select_fusion), calls=%async_computation.2 | async-start | bytes 262144 | tf_op jit(solution)/shard_map/all_to_all | solution.py:136
  119.1 11.7 %all-to-all-start.3 = ((f32[8,2,4096]{2,1,0:T(2,128)}), f32[8,2,4096]{2,1,0:T(2,128)S(1)}, u32[]{:S(2)}, u32[]{:S(2)}) async-start(f32[8,2,4096]{2,1,0:T(2,128)} %reshape.104), calls=%async_computation.3 | async-start | bytes 524288 | tf_op jit(solution)/shard_map/all_to_all | solution.py:142
where the time goes:
time: 136 us; the launch traced here: 135 us
  matrix products  43.3 us (32%)
  blocking collectives  39.2 us (29%)
  waiting for transfers between devices  19.8 us (15%)
  starting transfers between devices  17.7 us (13%)
  other arithmetic  8.12 us (6%)
  local copies, waits for them, and re-layouts  6.19 us (5%)
    all_gather x1, blocking collectives, local(): lax.all_gather(gated_out, 'expert', axis=0, tiled=True)  32.3 us
    dot_general x1, matrix products, expert_terms(): lax.dot_general(rows, up_weight, dims, preferred_element_type=jnp.float32)  11.3 us
    dot_general x1, matrix products, expert_terms(): lax.dot_general(rows, gate_weight, dims, preferred_element_type=jnp.float32)  11.3 us
    dot_general x1, matrix products, expert_terms(): jnp.dot(lower_hidden, down_weight, preferred_element_type=jnp.float32)  7.7 us
    dot_general x1, matrix products, expert_terms(): jnp.dot(upper_hidden, down_weight, preferred_element_type=jnp.float32)  7.7 us
    all_to_all x1, waiting for transfers between devices, local(): lax.all_to_all(partial_value, 'expert', split_axis=0, concat_axis=0, tile...  7.44 us
    all_to_all x1, waiting for transfers between devices, local(): lax.all_to_all(outgoing, 'expert', split_axis=0, concat_axis=0, tiled=True)  6.94 us
    all_to_all x1, starting transfers between devices, local(): lax.all_to_all(outgoing, 'expert', split_axis=0, concat_axis=0, tiled=True)  5.49 us
  transfers between devices with their start and end apart: 4, of which 4 were waited for; matrix products, arithmetic and copies ran while one was open for 4% of the time, Pallas kernels for 0%

commit v1 on v0

--- a/solution.py
+++ b/solution.py
@@ -107,7 +107,10 @@
         out_weight,
         preferred_element_type=jnp.float32,
     )
-    returned_cols = lax.all_to_all(columns, "expert", split_axis=0, concat_axis=1, tiled=True)
+    n_dev = lax.axis_size("expert")
+    blocks = jnp.stack(jnp.split(columns, n_dev, axis=0), axis=0)
+    blocks = lax.all_to_all(blocks, "expert", split_axis=0, concat_axis=0)
+    returned_cols = jnp.concatenate(blocks, axis=1)
     mixed = lax.psum(returned_cols, "tensor").astype(jnp.bfloat16)
     hidden_state = (residual.astype(jnp.float32) + mixed.astype(jnp.float32)).astype(jnp.bfloat16)
     wide = hidden_state.astype(jnp.float32)

time: 136 us -> 140 us (1.029)
  local copies, waits for them, and re-layouts: 6.19 us -> 10.3 us
    unnamed x6 -> x13, local copies, waits for them, and re-layouts: 2.47 us -> 6.65 us
where the time goes in v1:
time: 140 us; the launch traced here: 139 us
  matrix products  43.3 us (31%)
  blocking collectives  39.2 us (28%)
  waiting for transfers between devices  19.8 us (14%)
  starting transfers between devices  17.7 us (13%)
  local copies, waits for them, and re-layouts  10.3 us (7%)
  other arithmetic  8.12 us (6%)
    all_gather x1, blocking collectives, local(): lax.all_gather(gated_out, 'expert', axis=0, tiled=True)  32.3 us
    dot_general x1, matrix products, expert_terms(): lax.dot_general(rows, up_weight, dims, preferred_element_type=jnp.float32)  11.3 us
    dot_general x1, matrix products, expert_terms(): lax.dot_general(rows, gate_weight, dims, preferred_element_type=jnp.float32)  11.3 us
    dot_general x1, matrix products, expert_terms(): jnp.dot(lower_hidden, down_weight, preferred_element_type=jnp.float32)  7.7 us
    dot_general x1, matrix products, expert_terms(): jnp.dot(upper_hidden, down_weight, preferred_element_type=jnp.float32)  7.7 us
    all_to_all x1, waiting for transfers between devices, local(): lax.all_to_all(partial_value, 'expert', split_axis=0, concat_axis=0, tile...  7.44 us
    all_to_all x1, waiting for transfers between devices, local(): lax.all_to_all(outgoing, 'expert', split_axis=0, concat_axis=0, tiled=True)  6.94 us
    unnamed x13, local copies, waits for them, and re-layouts  6.65 us
  transfers between devices with their start and end apart: 4, of which 4 were waited for; matrix products, arithmetic and copies ran while one was open for 4% of the time, Pallas kernels for 0%

profile of v1, /device:TPU:0, one launch (start us, length us, event | category | flops | bytes accessed | tf_op | source)
XLA Modules:
  0.0 139.1 jit_solution(4682257001229779239)
XLA Ops:
  0.7 0.8 copy.67
  1.4 0.8 copy.65
  2.2 1.1 fusion.39
  3.3 1.0 exponential_negate_fusion
  4.3 0.7 broadcast_subtract_fusion
  4.9 1.0 fusion.32
  6.0 0.9 fusion.37
  6.9 1.1 fusion.38
  8.0 0.8 fusion.24
  8.8 32.3 %all-gather = bf16[8,2,4096]{2,1,0:T(2,128)(2,1)S(1)} all-gather(bf16[1,2,4096]{2,1,0:T(2,128)(2,1)S(1)} %fusion.24), channel_id=1, replica_groups=mesh['groups'=2,'expert'=8,'tensor'=2] {'expert'}, dimensions={0}, use_global_device_ids=true | all-gather | bytes 147456 | tf_op jit(solution)/shard_map/all_gather | solution.py:106
  41.2 2.8 %fusion.40 = f32[16,512]{1,0:T(8,128)S(1)} fusion(bf16[16,4096]{1,0:T(8,128)(2,1)S(1)} %reshape.111, bf16[4096,512]{1,0:T(8,128)(2,1)} %param.34), kind=kOutput, calls=%fused_computation.92 | convolution fusion | flops 67108864 | bytes 4358144 | tf_op jit(solution)/shard_map/dot_general | solution.py:105
  44.0 0.6 constant_dynamic-update-slice_fusion.7
  44.7 0.6 constant_dynamic-update-slice_fusion.6
  45.2 0.6 constant_dynamic-update-slice_fusion.5
  45.8 0.6 constant_dynamic-update-slice_fusion.4
  46.4 0.6 constant_dynamic-update-slice_fusion.3
  47.0 0.6 constant_dynamic-update-slice_fusion.2
  47.6 0.6 constant_dynamic-update-slice_fusion.1
  48.2 0.6 constant_dynamic-update-slice_fusion
  48.8 5.5 %all-to-all-start = ((f32[8,2,512]{2,1,0:T(2,128)}), f32[8,2,512]{2,1,0:T(2,128)S(1)}, u32[]{:S(2)}, u32[]{:S(2)}) async-start(f32[8,2,512]{2,1,0:T(2,128)} %constant_dynamic-update-slice_fusion), calls=%async_computation | async-start | bytes 65536 | tf_op jit(solution)/shard_map/all_to_all | solution.py:112
  54.3 0.7 convert_element_type.85
  55.0 0.8 convert_reduce_fusion
  55.7 0.2 convolution_compare_fusion
  55.9 0.1 copy.70
  56.0 5.0 %all-to-all-done = f32[8,2,512]{2,1,0:T(2,128)S(1)} async-done(((f32[8,2,512]{2,1,0:T(2,128)}), f32[8,2,512]{2,1,0:T(2,128)S(1)}, u32[]{:S(2)}, u32[]{:S(2)}) %all-to-all-start) | async-done | bytes 32800 | tf_op jit(solution)/shard_map/all_to_all | solution.py:112
  61.0 0.6 broadcast_in_dim.29
  61.6 3.3 %all-to-all-start.1 = ((bf16[8,2,3]{2,1,0:T(2,128)(2,1)}), bf16[8,2,3]{2,1,0:T(2,128)(2,1)S(1)}, u32[]{:S(2)}, u32[]{:S(2)}) async-start(bf16[8,2,3]{2,1,0:T(2,128)(2,1)} %broadcast_in_dim.29), calls=%async_computation.1 | async-start | bytes 8192 | tf_op jit(solution)/shard_map/all_to_all | solution.py:140
  64.9 3.4 %psum.14 = bf16[2,4096]{1,0:T(2,128)(2,1)S(1)} all-reduce(f32[2,4096]{1,0:T(2,128)S(1)} %bitcast.88), channel_id=1, replica_groups=mesh['groups'=2,'expert'=8,'tensor'=2] {'tensor'}, use_global_device_ids=true, to_apply=%region_1.2 | all-reduce | flops 8192 | bytes 49152 | tf_op jit(solution)/shard_map/psum | solution.py:114
  68.3 0.9 fusion.13
  69.2 0.8 fusion.15
  70.0 0.8 broadcast_select_fusion
  70.8 0.4 all-to-all-done.1
  71.2 5.5 %all-to-all-start.2 = ((bf16[8,2,4096]{2,1,0:T(2,128)(2,1)}), bf16[8,2,4096]{2,1,0:T(2,128)(2,1)S(1)}, u32[]{:S(2)}, u32[]{:S(2)}) async-start(bf16[8,2,4096]{2,1,0:T(2,128)(2,1)} %broadcast_select_fusion), calls=%async_computation.2 | async-start | bytes 262144 | tf_op jit(solution)/shard_map/all_to_all | solution.py:139
  76.8 0.1 copy.68
  76.9 0.1 fusion.27
  76.9 0.1 copy.71
  77.3 6.9 %all-to-all-done.2 = bf16[8,2,4096]{2,1,0:T(2,128)(2,1)S(1)} async-done(((bf16[8,2,4096]{2,1,0:T(2,128)(2,1)}), bf16[8,2,4096]{2,1,0:T(2,128)(2,1)S(1)}, u32[]{:S(2)}, u32[]{:S(2)}) %all-to-all-start.2) | async-done | bytes 131104 | tf_op jit(solution)/shard_map/all_to_all | solution.py:139
  84.3 11.3 %fusion.41 = f32[16,2304]{1,0:T(8,128)S(1)} fusion(bf16[16,4096]{1,0:T(8,128)(2,1)S(1)} %reshape.108, bf16[2304,4096]{1,0:T(8,128)(2,1)} %param.39), kind=kOutput, calls=%fused_computation.93 | convolution fusion | flops 301989888 | bytes 19152896 | tf_op jit(solution)/shard_map/dot_general | solution.py:40
  95.6 11.3 %fusion.2 = bf16[16,2304]{1,0:T(8,128)(2,1)S(1)} fusion(bf16[16,4096]{1,0:T(8,128)(2,1)S(1)} %reshape.108, bf16[2304,4096]{1,0:T(8,128)(2,1)} %param.40, f32[16,2304]{1,0:T(8,128)S(1)} %fusion.41), kind=kOutput, calls=%fused_computation.6 | convolution fusion | flops 302211072 | bytes 19226624 | tf_op jit(solution)/shard_map/dot_general | solution.py:41
  107.0 7.7 %convolution_multiply_fusion.2 = f32[16,4096]{1,0:T(8,128)S(1)} fusion(bf16[2304,4096]{1,0:T(8,128)(2,1)} %param.41, f32[16]{0:T(128)S(1)} %mul.245, bf16[16,2304]{1,0:T(8,128)(2,1)S(1)} %fusion.2, pred[2304]{0:T(1024)(128)(4,1)S(1)} %get-tuple-element.38), kind=kOutput, calls=%fused_computation.4 | convolution fusion | flops 302092288 | bytes 19212608 | tf_op jit(solution)/shard_map/dot_general | solution.py:56
  114.7 7.7 %fusion.1 = f32[16,4096]{1,0:T(8,128)S(1)} fusion(f32[16,4096]{1,0:T(8,128)S(1)} %convolution_multiply_fusion.2, bf16[2304,4096]{1,0:T(8,128)(2,1)} %param.41, f32[16]{0:T(128)S(1)} %mul.262, bf16[16,2304]{1,0:T(8,128)(2,1)S(1)} %fusion.2, pred[2304]{0:T(1024)(128)(4,1)S(1)} %get-tuple-element.37), kind=kOutput, calls=%fused_computation.3 | convolution fusion | flops 302157824 | bytes 19474752 | tf_op jit(solution)/shard_map/dot_general | solution.py:57
  122.4 0.8 reshape.109
  123.2 3.4 %all-to-all-start.3 = ((f32[8,2,4096]{2,1,0:T(2,128)}), f32[8,2,4096]{2,1,0:T(2,128)S(1)}, u32[]{:S(2)}, u32[]{:S(2)}) async-start(f32[8,2,4096]{2,1,0:T(2,128)} %reshape.109), calls=%async_computation.3 | async-start | bytes 524288 | tf_op jit(solution)/shard_map/all_to_all | solution.py:145
  126.6 0.9 copy.72
  127.5 7.4 %all-to-all-done.3 = f32[8,2,4096]{2,1,0:T(2,128)S(1)} async-done(((f32[8,2,4096]{2,1,0:T(2,128)}), f32[8,2,4096]{2,1,0:T(2,128)S(1)}, u32[]{:S(2)}, u32[]{:S(2)}) %all-to-all-start.3) | async-done | bytes 262176 | tf_op jit(solution)/shard_map/all_to_all | solution.py:145
  134.9 0.1 reduce_sum.69
  135.0 3.4 %psum.15 = f32[2,4096]{1,0:T(2,128)S(1)} all-reduce(f32[2,4096]{1,0:T(2,128)S(1)} %reduce_sum.69), channel_id=1, replica_groups=mesh['groups'=2,'expert'=8,'tensor'=2] {'tensor'}, use_global_device_ids=true, to_apply=%region_8.9 | all-reduce | flops 8192 | bytes 65536 | tf_op jit(solution)/shard_map/psum | solution.py:146
  138.4 0.6 fusion.16
  (12 shorter events, 0.4 us)
Async XLA Ops:
  0.6 6.3 %copy-start = (bf16[2,16,4096]{2,1,0:T(8,128)(2,1)S(1)}, bf16[2,16,4096]{2,1,0:T(8,128)(2,1)}, u32[]{:S(2)}) copy-start(bf16[2,16,4096]{2,1,0:T(8,128)(2,1)} %param.27) | copy-start | bytes 786436
  48.8 12.1 %all-to-all-start = ((f32[8,2,512]{2,1,0:T(2,128)}), f32[8,2,512]{2,1,0:T(2,128)S(1)}, u32[]{:S(2)}, u32[]{:S(2)}) async-start(f32[8,2,512]{2,1,0:T(2,128)} %constant_dynamic-update-slice_fusion), calls=%async_computation | async-start | bytes 65536 | tf_op jit(solution)/shard_map/all_to_all | solution.py:112
  61.6 9.7 %all-to-all-start.1 = ((bf16[8,2,3]{2,1,0:T(2,128)(2,1)}), bf16[8,2,3]{2,1,0:T(2,128)(2,1)S(1)}, u32[]{:S(2)}, u32[]{:S(2)}) async-start(bf16[8,2,3]{2,1,0:T(2,128)(2,1)} %broadcast_in_dim.29), calls=%async_computation.1 | async-start | bytes 8192 | tf_op jit(solution)/shard_map/all_to_all | solution.py:140
  71.2 13.0 %all-to-all-start.2 = ((bf16[8,2,4096]{2,1,0:T(2,128)(2,1)}), bf16[8,2,4096]{2,1,0:T(2,128)(2,1)S(1)}, u32[]{:S(2)}, u32[]{:S(2)}) async-start(bf16[8,2,4096]{2,1,0:T(2,128)(2,1)} %broadcast_select_fusion), calls=%async_computation.2 | async-start | bytes 262144 | tf_op jit(solution)/shard_map/all_to_all | solution.py:139
  123.2 11.7 %all-to-all-start.3 = ((f32[8,2,4096]{2,1,0:T(2,128)}), f32[8,2,4096]{2,1,0:T(2,128)S(1)}, u32[]{:S(2)}, u32[]{:S(2)}) async-start(f32[8,2,4096]{2,1,0:T(2,128)} %reshape.109), calls=%async_computation.3 | async-start | bytes 524288 | tf_op jit(solution)/shard_map/all_to_all | solution.py:145
